TPU v7x, 32 devices: a whole 2x2x4 slice. The times are simulated.
32 devices in a mesh: seq: 16 (over z, y, x), head: 2 (over core).
Axes of the slice: x: 2, y: 2, z: 4, core: 2. Of those that a mesh axis runs over, the one named last changes fastest.
Arguments:
- attn_q: bfloat16 [2048, 512], P('seq', 'head'), may hold values from -6 to 6
- attn_k: bfloat16 [2048, 512], P('seq', 'head'), may hold values from -6 to 6
- attn_v: bfloat16 [2048, 512], P('seq', 'head'), may hold values from -6 to 6
- attn_out: bfloat16 [2048, 512], P('seq', 'head'), may hold values from -0.29882812 to 0.29882812
- attn_dout: bfloat16 [2048, 512], P('seq', 'head'), may hold values from -96 to 96
- attn_lse: float32 [4, 2048], P('head', 'seq'), may hold values from 7 to 8
- w_kv: bfloat16 [512, 2, 512], P('seq', None, 'head'), may hold values from -0.25 to 0.25
- gdn_q: bfloat16 [2048, 512], P('seq', 'head'), may hold values from -6 to 6
- gdn_k: bfloat16 [2048, 512], P('seq', 'head'), may hold values from -6 to 6
- gdn_v: bfloat16 [2048, 512], P('seq', 'head'), may hold values from -6 to 6
- gdn_dout: bfloat16 [2048, 512], P('seq', 'head'), may hold values from -6 to 6
- gdn_log_decay: float32 [4, 2048], P('head', 'seq'), may hold values from -0.56 to 0
- gdn_beta: float32 [4, 2048], P('head', 'seq'), may hold values from 0 to 0.9
- gdn_states: float32 [32, 4, 128, 128], P('seq', 'head'), may hold values from -24 to 24
Outputs:
- attn_dq: bfloat16 [2048, 512], P('seq', 'head')
- attn_dx: bfloat16 [512, 2048], P('head', 'seq')
- gdn_dq: bfloat16 [2048, 512], P('seq', 'head')
- gdn_dk: bfloat16 [2048, 512], P('seq', 'head')
- gdn_dv: bfloat16 [2048, 512], P('seq', 'head')
- gdn_dlog_decay: float32 [4, 2048], P('head', 'seq')
- gdn_dbeta: float32 [4, 2048], P('head', 'seq')
All inputs are finite; a program needn't handle non-finite values.
Results may differ from a plain program's by a relative error of at most 0.0078.
Values may be sent and summed in bfloat16 or wider, within the bound.
A program may use at most 64 MiB of HBM per device.

v0:
```python
import jax
import jax.numpy as jnp
from jax import lax
from jax.sharding import PartitionSpec as P

BLOCK = 64
WINDOW = 1024
HIGH = lax.Precision.HIGHEST


def from_behind(block, axis, distance):
    devices = range(lax.axis_size(axis))
    route = [(i - distance, i) for i in devices if i - distance in devices]
    return lax.ppermute(block, axis, route)


def matmul(left_side, right_side):
    return jnp.dot(left_side, right_side, precision=HIGH)


def stack_mul(left_side, right_side):
    return jnp.einsum("hij,hjk->hik", left_side, right_side, precision=HIGH)


def unit_rows(matrix):
    return matrix * lax.rsqrt(jnp.sum(matrix * matrix, axis=-1, keepdims=True) + 1e-06)


def inverse_unit(lower_part):
    length = lower_part.shape[0]
    identity = jnp.eye(length, dtype=jnp.float32)
    powered = lower_part
    result = identity - lower_part
    for _ in range(length.bit_length() - 2):
        powered = matmul(powered, powered)
        result = matmul(result, identity + powered)
    return result


def block_parts(queries, keys_in, decays, strengths):
    length, depth = queries.shape
    unit_q = unit_rows(queries) * depth ** (-0.5)
    unit_k = unit_rows(keys_in)
    summed = jnp.cumsum(decays)
    row_ids = lax.broadcasted_iota(jnp.int32, (length, length), 0)
    col_ids = lax.broadcasted_iota(jnp.int32, (length, length), 1)
    causal = row_ids >= col_ids
    fading = jnp.where(
        causal, jnp.exp(jnp.where(causal, summed[:, None] - summed[None, :], 0.0)), 0.0
    )
    strict = jnp.where(row_ids > col_ids, fading, 0.0)
    lower_part = strengths[:, None] * strict * matmul(unit_k, unit_k.T)
    solved = inverse_unit(lower_part)
    growth = jnp.exp(summed)
    widened = matmul(solved, (strengths * growth)[:, None] * unit_k)
    attention = fading * matmul(unit_q, unit_k.T)
    tailing = jnp.exp(summed[-1] - summed)[:, None] * unit_k
    return (unit_q, solved, growth, widened, attention, tailing)


def block_forward(queries, keys_in, values, decays, strengths, initial):
    unit_q, solved, growth, widened, attention, tailing = block_parts(
        queries, keys_in, decays, strengths
    )
    fresh = matmul(solved, strengths[:, None] * values) - matmul(widened, initial)
    output = growth[:, None] * matmul(unit_q, initial) + matmul(attention, fresh)
    final = growth[-1] * initial + matmul(tailing.T, fresh)
    return (output, final)


def block_adjoint(queries, keys_in, decays, strengths, out_grad):
    unit_q, solved, growth, widened, attention, tailing = block_parts(
        queries, keys_in, decays, strengths
    )
    depth = queries.shape[1]
    carry_map = growth[-1] * jnp.eye(depth, dtype=jnp.float32) - matmul(widened.T, tailing)
    local_term = matmul((growth[:, None] * unit_q).T, out_grad) - matmul(
        widened.T, matmul(attention.T, out_grad)
    )
    return (carry_map, local_term)


def block_grads(queries, keys_in, values, decays, strengths, initial, out_grad, later_adjoint):
    _, pullback = jax.vjp(block_forward, queries, keys_in, values, decays, strengths, initial)
    grad_q, grad_k, grad_v, grad_decay, grad_beta, _ = pullback((out_grad, later_adjoint))
    return (grad_q, grad_k, grad_v, grad_decay, grad_beta)


def window_terms(queries, keys_in, values, out_grad, log_totals, dot_terms, query_pos, key_pos):
    scaling = queries.shape[2] ** (-0.5)
    logits = (
        jnp.einsum("rhd,khd->hrk", queries, keys_in, preferred_element_type=jnp.float32) * scaling
    )
    distance = query_pos[:, None] - key_pos[None, :]
    visible = ((distance >= 0) & (distance < WINDOW) & (key_pos[None, :] >= 0))[None, :, :]
    chances = jnp.where(
        visible, jnp.exp(jnp.where(visible, logits - log_totals[:, :, None], 0.0)), 0.0
    )
    grad_prob = jnp.einsum("rhd,khd->hrk", out_grad, values, preferred_element_type=jnp.float32)
    grad_logit = (chances * (grad_prob - dot_terms[:, :, None])).astype(jnp.bfloat16)
    weights = chances.astype(jnp.bfloat16)
    grad_q = (
        jnp.einsum("hrk,khd->rhd", grad_logit, keys_in, preferred_element_type=jnp.float32)
        * scaling
    )
    grad_k = (
        jnp.einsum("hrk,rhd->khd", grad_logit, queries, preferred_element_type=jnp.float32)
        * scaling
    )
    grad_v = jnp.einsum("hrk,rhd->khd", weights, out_grad, preferred_element_type=jnp.float32)
    return (grad_q, grad_k, grad_v)


def per_device(
    attn_q,
    attn_k,
    attn_v,
    attn_out,
    attn_dout,
    attn_lse,
    w_kv,
    gdn_q,
    gdn_k,
    gdn_v,
    gdn_dout,
    gdn_log_decay,
    gdn_beta,
    gdn_states,
):
    row_count, column_count = attn_q.shape
    head_count = attn_lse.shape[0]
    depth = column_count // head_count
    reach_count = WINDOW // row_count
    position = lax.axis_index("seq")

    def by_heads(matrix):
        return matrix.reshape(-1, head_count, depth)

    dot_terms = jnp.sum(
        by_heads(attn_dout).astype(jnp.float32) * by_heads(attn_out).astype(jnp.float32), axis=2
    ).T
    query_pos = position * row_count + jnp.arange(row_count, dtype=jnp.int32)
    couple = jnp.stack([attn_k, attn_v])
    pieces = []
    for offset_by in range(reach_count, 0, -1):
        pieces.append(from_behind(couple, "seq", offset_by))
    before = jnp.concatenate(pieces, axis=1)
    window = jnp.concatenate([before, couple], axis=1)
    key_pos = (position - reach_count) * row_count + jnp.arange(
        (reach_count + 1) * row_count, dtype=jnp.int32
    )
    grad_q, grad_k, grad_v = window_terms(
        by_heads(attn_q),
        by_heads(window[0]),
        by_heads(window[1]),
        by_heads(attn_dout),
        attn_lse,
        dot_terms,
        query_pos,
        key_pos,
    )
    own_rows = jnp.stack([attn_q, attn_dout])
    own_stats = jnp.stack([attn_lse, dot_terms])
    query_parts = [own_rows]
    stat_parts = [own_stats]
    for offset_by in range(1, reach_count + 1):
        query_parts.append(from_behind(own_rows, "seq", -offset_by))
        stat_parts.append(from_behind(own_stats, "seq", -offset_by))
    later_rows = jnp.concatenate(query_parts, axis=1)
    later_stats = jnp.concatenate(stat_parts, axis=2)
    later_pos = position * row_count + jnp.arange((reach_count + 1) * row_count, dtype=jnp.int32)
    _, own_k, own_v = window_terms(
        by_heads(later_rows[0]),
        by_heads(attn_k),
        by_heads(attn_v),
        by_heads(later_rows[1]),
        later_stats[0],
        later_stats[1],
        later_pos,
        query_pos,
    )
    key_grad = own_k.reshape(row_count, column_count).astype(jnp.bfloat16)
    value_grad = own_v.reshape(row_count, column_count).astype(jnp.bfloat16)
    attn_dq = grad_q.reshape(row_count, column_count).astype(jnp.bfloat16)
    row_piece = lax.all_gather(w_kv, "seq", axis=0, tiled=True)
    from_keys = lax.dot_general(
        row_piece[:, 0, :], key_grad, (((1,), (1,)), ((), ())), preferred_element_type=jnp.float32
    )
    partial_value = from_keys + lax.dot_general(
        row_piece[:, 1, :], value_grad, (((1,), (1,)), ((), ())), preferred_element_type=jnp.float32
    )
    attn_dx = lax.psum_scatter(partial_value, "head", scatter_dimension=0, tiled=True).astype(
        jnp.bfloat16
    )
    block_count = row_count // BLOCK

    def by_blocks(matrix):
        return (
            matrix.reshape(block_count, BLOCK, head_count, depth)
            .transpose(0, 2, 1, 3)
            .astype(jnp.float32)
        )

    def gates_by_blocks(matrix):
        return matrix.reshape(head_count, block_count, BLOCK).transpose(1, 0, 2)

    queries = by_blocks(gdn_q)
    keys_in = by_blocks(gdn_k)
    values = by_blocks(gdn_v)
    out_grad = by_blocks(gdn_dout)
    decays = gates_by_blocks(gdn_log_decay)
    strengths = gates_by_blocks(gdn_beta)
    carry_map, local_term = jax.vmap(jax.vmap(block_adjoint))(
        queries, keys_in, decays, strengths, out_grad
    )
    identity = jnp.broadcast_to(jnp.eye(depth, dtype=jnp.float32), (head_count, depth, depth))
    nothing = jnp.zeros((head_count, depth, depth), jnp.float32)

    def compose_blocks(carry, couple_in):
        across, offset = carry
        return (
            (stack_mul(couple_in[0], across), stack_mul(couple_in[0], offset) + couple_in[1]),
            None,
        )

    (across, offset), _ = lax.scan(
        compose_blocks, (identity, nothing), (carry_map, local_term), reverse=True
    )

    def relay_step(step_no, incoming):
        return from_behind(stack_mul(across, incoming) + offset, "seq", -1)

    carried = lax.fori_loop(0, lax.axis_size("seq") - 1, relay_step, nothing)

    def backward(carry, couple_in):
        return (stack_mul(couple_in[0], carry) + couple_in[1], carry)

    _, later_adjoint = lax.scan(backward, carried, (carry_map, local_term), reverse=True)
    grad_bq, grad_bk, grad_bv, grad_decay, grad_beta = jax.vmap(jax.vmap(block_grads))(
        queries, keys_in, values, decays, strengths, gdn_states, out_grad, later_adjoint
    )

    def tokens_back(stacked):
        return stacked.transpose(0, 2, 1, 3).reshape(row_count, column_count).astype(jnp.bfloat16)

    def per_head(stacked):
        return stacked.transpose(1, 0, 2).reshape(head_count, row_count)

    return (
        attn_dq,
        attn_dx,
        tokens_back(grad_bq),
        tokens_back(grad_bk),
        tokens_back(grad_bv),
        per_head(grad_decay),
        per_head(grad_beta),
    )


def solution(mesh):
    placed = (
        P("seq", "head"),
        P("seq", "head"),
        P("seq", "head"),
        P("seq", "head"),
        P("seq", "head"),
        P("head", "seq"),
        P("seq", None, "head"),
        P("seq", "head"),
        P("seq", "head"),
        P("seq", "head"),
        P("seq", "head"),
        P("head", "seq"),
        P("head", "seq"),
        P("seq", "head", None, None),
    )
    return jax.shard_map(
        per_device,
        mesh=mesh,
        in_specs=placed,
        out_specs=(
            P("seq", "head"),
            P("head", "seq"),
            P("seq", "head"),
            P("seq", "head"),
            P("seq", "head"),
            P("head", "seq"),
            P("head", "seq"),
        ),
        check_vma=False,
    )
```

profile of v0, /device:TPU:0, one launch (start us, length us, event | category | flops | bytes accessed | tf_op | source)
XLA Modules:
  0.0 311.4 jit_solution(4315394593394781818)
XLA Ops:
  25.4 1.3 fusion.50
  30.9 133.4 %while.43 = (s32[]{:T(128)}, f32[2,128,128]{2,1,0:T(8,128)S(1)}, f32[2,128,128]{2,1,0:T(8,128)S(1)}, f32[2,128,128]{2,1,0:T(8,128)S(1)}, s32[]{:T(128)}) while((s32[]{:T(128)}, f32[2,128,128]{2,1,0:T(8,128)S(1)}, f32[2,128,128]{2,1,0:T(8,128)S(1)}, f32[2,128,128]{2,1,0:T(8,128)S(1)}, s32[]{:T(128)}) %tuple.116), condition=%wide.region_9.10_spmd, body=%wide.region_8.9_spmd.sunk | while | flops 50364416 | bytes 1048677 | solution.py:233
  32.5 7.7 %collective-permute-done = f32[2,128,128]{2,1,0:T(8,128)S(1)} collective-permute-done((f32[2,128,128]{2,1,0:T(8,128)S(1)}, f32[2,128,128]{2,1,0:T(8,128)S(1)}, u32[]{:S(2)}, u32[]{:S(2)}) %collective-permute-start) | collective-permute-done | bytes 131104 | tf_op jit(solution)/shard_map/while/body/eval_jaxpr/ppermute | solution.py:14
  41.8 6.8 %collective-permute-done = f32[2,128,128]{2,1,0:T(8,128)S(1)} collective-permute-done((f32[2,128,128]{2,1,0:T(8,128)S(1)}, f32[2,128,128]{2,1,0:T(8,128)S(1)}, u32[]{:S(2)}, u32[]{:S(2)}) %collective-permute-start) | collective-permute-done | bytes 131104 | tf_op jit(solution)/shard_map/while/body/eval_jaxpr/ppermute | solution.py:14
  48.8 1.3 collective-permute-start
  50.1 6.5 %collective-permute-done = f32[2,128,128]{2,1,0:T(8,128)S(1)} collective-permute-done((f32[2,128,128]{2,1,0:T(8,128)S(1)}, f32[2,128,128]{2,1,0:T(8,128)S(1)}, u32[]{:S(2)}, u32[]{:S(2)}) %collective-permute-start) | collective-permute-done | bytes 131104 | tf_op jit(solution)/shard_map/while/body/eval_jaxpr/ppermute | solution.py:14
  58.2 6.5 %collective-permute-done = f32[2,128,128]{2,1,0:T(8,128)S(1)} collective-permute-done((f32[2,128,128]{2,1,0:T(8,128)S(1)}, f32[2,128,128]{2,1,0:T(8,128)S(1)}, u32[]{:S(2)}, u32[]{:S(2)}) %collective-permute-start) | collective-permute-done | bytes 131104 | tf_op jit(solution)/shard_map/while/body/eval_jaxpr/ppermute | solution.py:14
  66.2 6.9 %collective-permute-done = f32[2,128,128]{2,1,0:T(8,128)S(1)} collective-permute-done((f32[2,128,128]{2,1,0:T(8,128)S(1)}, f32[2,128,128]{2,1,0:T(8,128)S(1)}, u32[]{:S(2)}, u32[]{:S(2)}) %collective-permute-start) | collective-permute-done | bytes 131104 | tf_op jit(solution)/shard_map/while/body/eval_jaxpr/ppermute | solution.py:14
  74.7 7.4 %collective-permute-done = f32[2,128,128]{2,1,0:T(8,128)S(1)} collective-permute-done((f32[2,128,128]{2,1,0:T(8,128)S(1)}, f32[2,128,128]{2,1,0:T(8,128)S(1)}, u32[]{:S(2)}, u32[]{:S(2)}) %collective-permute-start) | collective-permute-done | bytes 131104 | tf_op jit(solution)/shard_map/while/body/eval_jaxpr/ppermute | solution.py:14
  83.6 8.7 %collective-permute-done = f32[2,128,128]{2,1,0:T(8,128)S(1)} collective-permute-done((f32[2,128,128]{2,1,0:T(8,128)S(1)}, f32[2,128,128]{2,1,0:T(8,128)S(1)}, u32[]{:S(2)}, u32[]{:S(2)}) %collective-permute-start) | collective-permute-done | bytes 131104 | tf_op jit(solution)/shard_map/while/body/eval_jaxpr/ppermute | solution.py:14
  93.8 8.7 %collective-permute-done = f32[2,128,128]{2,1,0:T(8,128)S(1)} collective-permute-done((f32[2,128,128]{2,1,0:T(8,128)S(1)}, f32[2,128,128]{2,1,0:T(8,128)S(1)}, u32[]{:S(2)}, u32[]{:S(2)}) %collective-permute-start) | collective-permute-done | bytes 131104 | tf_op jit(solution)/shard_map/while/body/eval_jaxpr/ppermute | solution.py:14
  104.2 7.2 %collective-permute-done = f32[2,128,128]{2,1,0:T(8,128)S(1)} collective-permute-done((f32[2,128,128]{2,1,0:T(8,128)S(1)}, f32[2,128,128]{2,1,0:T(8,128)S(1)}, u32[]{:S(2)}, u32[]{:S(2)}) %collective-permute-start) | collective-permute-done | bytes 131104 | tf_op jit(solution)/shard_map/while/body/eval_jaxpr/ppermute | solution.py:14
  112.9 6.8 %collective-permute-done = f32[2,128,128]{2,1,0:T(8,128)S(1)} collective-permute-done((f32[2,128,128]{2,1,0:T(8,128)S(1)}, f32[2,128,128]{2,1,0:T(8,128)S(1)}, u32[]{:S(2)}, u32[]{:S(2)}) %collective-permute-start) | collective-permute-done | bytes 131104 | tf_op jit(solution)/shard_map/while/body/eval_jaxpr/ppermute | solution.py:14
  121.3 7.1 %collective-permute-done = f32[2,128,128]{2,1,0:T(8,128)S(1)} collective-permute-done((f32[2,128,128]{2,1,0:T(8,128)S(1)}, f32[2,128,128]{2,1,0:T(8,128)S(1)}, u32[]{:S(2)}, u32[]{:S(2)}) %collective-permute-start) | collective-permute-done | bytes 131104 | tf_op jit(solution)/shard_map/while/body/eval_jaxpr/ppermute | solution.py:14
  130.0 7.4 %collective-permute-done = f32[2,128,128]{2,1,0:T(8,128)S(1)} collective-permute-done((f32[2,128,128]{2,1,0:T(8,128)S(1)}, f32[2,128,128]{2,1,0:T(8,128)S(1)}, u32[]{:S(2)}, u32[]{:S(2)}) %collective-permute-start) | collective-permute-done | bytes 131104 | tf_op jit(solution)/shard_map/while/body/eval_jaxpr/ppermute | solution.py:14
  138.9 7.4 %collective-permute-done = f32[2,128,128]{2,1,0:T(8,128)S(1)} collective-permute-done((f32[2,128,128]{2,1,0:T(8,128)S(1)}, f32[2,128,128]{2,1,0:T(8,128)S(1)}, u32[]{:S(2)}, u32[]{:S(2)}) %collective-permute-start) | collective-permute-done | bytes 131104 | tf_op jit(solution)/shard_map/while/body/eval_jaxpr/ppermute | solution.py:14
  147.8 7.4 %collective-permute-done = f32[2,128,128]{2,1,0:T(8,128)S(1)} collective-permute-done((f32[2,128,128]{2,1,0:T(8,128)S(1)}, f32[2,128,128]{2,1,0:T(8,128)S(1)}, u32[]{:S(2)}, u32[]{:S(2)}) %collective-permute-start) | collective-permute-done | bytes 131104 | tf_op jit(solution)/shard_map/while/body/eval_jaxpr/ppermute | solution.py:14
  156.8 7.5 %collective-permute-done = f32[2,128,128]{2,1,0:T(8,128)S(1)} collective-permute-done((f32[2,128,128]{2,1,0:T(8,128)S(1)}, f32[2,128,128]{2,1,0:T(8,128)S(1)}, u32[]{:S(2)}, u32[]{:S(2)}) %collective-permute-start) | collective-permute-done | bytes 131104 | tf_op jit(solution)/shard_map/while/body/eval_jaxpr/ppermute | solution.py:14
  164.3 1.5 collective-permute-start.21
  180.5 54.2 %all_gather.3 = bf16[512,2,256]{2,0,1:T(8,128)(2,1)S(1)} all-gather(bf16[32,2,256]{2,0,1:T(8,128)(2,1)S(1)} %copy.284), channel_id=1, replica_groups=mesh['seq'=16,'head'=2] {'seq'}, dimensions={0}, use_global_device_ids=true | all-gather | bytes 557056 | tf_op jit(solution)/shard_map/all_gather | solution.py:185
  236.6 1.4 fusion.41
  242.9 1.3 collective-permute-start.22
  244.3 1.5 collective-permute-start.23
  257.5 1.9 collective-permute-done.11
  260.7 10.6 %collective-permute-start.1 = (bf16[2,128,256]{1,2,0:T(8,128)(2,1)S(1)}, bf16[2,128,256]{1,2,0:T(8,128)(2,1)}, u32[]{:S(2)}, u32[]{:S(2)}) collective-permute-start(bf16[2,128,256]{1,2,0:T(8,128)(2,1)S(1)} %pad_maximum_fusion), channel_id=1, source_target_pairs={{0,16},{2,18},{4,20},{6,22},{8,24},{10,26},{12,28},{14,30},{1,17},... | collective-permute-start | bytes 393224 | tf_op jit(solution)/shard_map/ppermute | solution.py:14
  271.3 6.4 %collective-permute-start.2 = (bf16[2,128,256]{1,2,0:T(8,128)(2,1)S(1)}, bf16[2,128,256]{1,2,0:T(8,128)(2,1)}, u32[]{:S(2)}, u32[]{:S(2)}) collective-permute-start(bf16[2,128,256]{1,2,0:T(8,128)(2,1)S(1)} %pad_maximum_fusion), channel_id=1, source_target_pairs={{0,14},{2,16},{4,18},{6,20},{8,22},{10,24},{12,26},{14,28},{16,30}... | collective-permute-start | bytes 393224 | tf_op jit(solution)/shard_map/ppermute | solution.py:14
  277.7 1.9 collective-permute-start.3
  279.7 2.0 collective-permute-start.4
  281.7 1.9 collective-permute-start.5
  287.8 3.0 collective-permute-start.6
  291.8 1.3 collective-permute-start.7
  294.0 3.1 collective-permute-start.8
  (307 shorter events, 93.0 us)
Async XLA Ops:
  7.2 295.8 %reduce-scatter.2.cloned.1.call-start = ((), (), s32[]{:S(2)}) async-start(), calls=%async_computation.1 | async-start | bytes 393216 | tf_op jit(solution)/shard_map/reduce_scatter | solution.py:192
  10.0 232.9 %collective-permute-start.17 = (f32[2,2,128]{2,1,0:T(2,128)S(1)}, f32[2,2,128]{2,1,0:T(2,128)S(1)}, u32[]{:S(2)}, u32[]{:S(2)}) collective-permute-start(f32[2,2,128]{2,1,0:T(2,128)S(1)} %get-tuple-element.350), channel_id=1, source_target_pairs={{2,0},{4,2},{6,4},{8,6},{10,8},{12,10},{14,12},{16,14},{18,16},{20... | collective-permute-start | bytes 6152 | tf_op jit(solution)/shard_map/ppermute | solution.py:14
  11.3 233.0 %collective-permute-start.18 = (f32[2,2,128]{2,1,0:T(2,128)S(1)}, f32[2,2,128]{2,1,0:T(2,128)S(1)}, u32[]{:S(2)}, u32[]{:S(2)}) collective-permute-start(f32[2,2,128]{2,1,0:T(2,128)S(1)} %get-tuple-element.350), channel_id=1, source_target_pairs={{4,0},{6,2},{8,4},{10,6},{12,8},{14,10},{16,12},{18,14},{20,16},{2... | collective-permute-start | bytes 6152 | tf_op jit(solution)/shard_map/ppermute | solution.py:14
  12.6 233.2 %collective-permute-start.19 = (f32[2,2,128]{2,1,0:T(2,128)S(1)}, f32[2,2,128]{2,1,0:T(2,128)S(1)}, u32[]{:S(2)}, u32[]{:S(2)}) collective-permute-start(f32[2,2,128]{2,1,0:T(2,128)S(1)} %get-tuple-element.350), channel_id=1, source_target_pairs={{6,0},{8,2},{10,4},{12,6},{14,8},{16,10},{18,12},{20,14},{22,16},{... | collective-permute-start | bytes 6152 | tf_op jit(solution)/shard_map/ppermute | solution.py:14
  13.9 233.2 %collective-permute-start.20 = (f32[2,2,128]{2,1,0:T(2,128)S(1)}, f32[2,2,128]{2,1,0:T(2,128)S(1)}, u32[]{:S(2)}, u32[]{:S(2)}) collective-permute-start(f32[2,2,128]{2,1,0:T(2,128)S(1)} %get-tuple-element.350), channel_id=1, source_target_pairs={{8,0},{10,2},{12,4},{14,6},{16,8},{18,10},{20,12},{22,14},{24,16},... | collective-permute-start | bytes 6152 | tf_op jit(solution)/shard_map/ppermute | solution.py:14
  31.2 9.0 %collective-permute-start = (f32[2,128,128]{2,1,0:T(8,128)S(1)}, f32[2,128,128]{2,1,0:T(8,128)S(1)}, u32[]{:S(2)}, u32[]{:S(2)}) collective-permute-start(f32[2,128,128]{2,1,0:T(8,128)S(1)} %convolution_add_fusion.20), channel_id=1, source_target_pairs={{2,0},{4,2},{6,4},{8,6},{10,8},{12,10},{14,12},{16,14},{18,16},{20... | collective-permute-start | bytes 393224 | tf_op jit(solution)/shard_map/while/body/eval_jaxpr/ppermute | solution.py:14
  40.4 8.1 %collective-permute-start = (f32[2,128,128]{2,1,0:T(8,128)S(1)}, f32[2,128,128]{2,1,0:T(8,128)S(1)}, u32[]{:S(2)}, u32[]{:S(2)}) collective-permute-start(f32[2,128,128]{2,1,0:T(8,128)S(1)} %convolution_add_fusion.20), channel_id=1, source_target_pairs={{2,0},{4,2},{6,4},{8,6},{10,8},{12,10},{14,12},{16,14},{18,16},{20... | collective-permute-start | bytes 393224 | tf_op jit(solution)/shard_map/while/body/eval_jaxpr/ppermute | solution.py:14
  64.9 8.2 %collective-permute-start = (f32[2,128,128]{2,1,0:T(8,128)S(1)}, f32[2,128,128]{2,1,0:T(8,128)S(1)}, u32[]{:S(2)}, u32[]{:S(2)}) collective-permute-start(f32[2,128,128]{2,1,0:T(8,128)S(1)} %convolution_add_fusion.20), channel_id=1, source_target_pairs={{2,0},{4,2},{6,4},{8,6},{10,8},{12,10},{14,12},{16,14},{18,16},{20... | collective-permute-start | bytes 393224 | tf_op jit(solution)/shard_map/while/body/eval_jaxpr/ppermute | solution.py:14
  73.4 8.7 %collective-permute-start = (f32[2,128,128]{2,1,0:T(8,128)S(1)}, f32[2,128,128]{2,1,0:T(8,128)S(1)}, u32[]{:S(2)}, u32[]{:S(2)}) collective-permute-start(f32[2,128,128]{2,1,0:T(8,128)S(1)} %convolution_add_fusion.20), channel_id=1, source_target_pairs={{2,0},{4,2},{6,4},{8,6},{10,8},{12,10},{14,12},{16,14},{18,16},{20... | collective-permute-start | bytes 393224 | tf_op jit(solution)/shard_map/while/body/eval_jaxpr/ppermute | solution.py:14
  82.3 10.0 %collective-permute-start = (f32[2,128,128]{2,1,0:T(8,128)S(1)}, f32[2,128,128]{2,1,0:T(8,128)S(1)}, u32[]{:S(2)}, u32[]{:S(2)}) collective-permute-start(f32[2,128,128]{2,1,0:T(8,128)S(1)} %convolution_add_fusion.20), channel_id=1, source_target_pairs={{2,0},{4,2},{6,4},{8,6},{10,8},{12,10},{14,12},{16,14},{18,16},{20... | collective-permute-start | bytes 393224 | tf_op jit(solution)/shard_map/while/body/eval_jaxpr/ppermute | solution.py:14
  92.5 10.0 %collective-permute-start = (f32[2,128,128]{2,1,0:T(8,128)S(1)}, f32[2,128,128]{2,1,0:T(8,128)S(1)}, u32[]{:S(2)}, u32[]{:S(2)}) collective-permute-start(f32[2,128,128]{2,1,0:T(8,128)S(1)} %convolution_add_fusion.20), channel_id=1, source_target_pairs={{2,0},{4,2},{6,4},{8,6},{10,8},{12,10},{14,12},{16,14},{18,16},{20... | collective-permute-start | bytes 393224 | tf_op jit(solution)/shard_map/while/body/eval_jaxpr/ppermute | solution.py:14
  102.9 8.5 %collective-permute-start = (f32[2,128,128]{2,1,0:T(8,128)S(1)}, f32[2,128,128]{2,1,0:T(8,128)S(1)}, u32[]{:S(2)}, u32[]{:S(2)}) collective-permute-start(f32[2,128,128]{2,1,0:T(8,128)S(1)} %convolution_add_fusion.20), channel_id=1, source_target_pairs={{2,0},{4,2},{6,4},{8,6},{10,8},{12,10},{14,12},{16,14},{18,16},{20... | collective-permute-start | bytes 393224 | tf_op jit(solution)/shard_map/while/body/eval_jaxpr/ppermute | solution.py:14
  111.6 8.1 %collective-permute-start = (f32[2,128,128]{2,1,0:T(8,128)S(1)}, f32[2,128,128]{2,1,0:T(8,128)S(1)}, u32[]{:S(2)}, u32[]{:S(2)}) collective-permute-start(f32[2,128,128]{2,1,0:T(8,128)S(1)} %convolution_add_fusion.20), channel_id=1, source_target_pairs={{2,0},{4,2},{6,4},{8,6},{10,8},{12,10},{14,12},{16,14},{18,16},{20... | collective-permute-start | bytes 393224 | tf_op jit(solution)/shard_map/while/body/eval_jaxpr/ppermute | solution.py:14
  120.0 8.4 %collective-permute-start = (f32[2,128,128]{2,1,0:T(8,128)S(1)}, f32[2,128,128]{2,1,0:T(8,128)S(1)}, u32[]{:S(2)}, u32[]{:S(2)}) collective-permute-start(f32[2,128,128]{2,1,0:T(8,128)S(1)} %convolution_add_fusion.20), channel_id=1, source_target_pairs={{2,0},{4,2},{6,4},{8,6},{10,8},{12,10},{14,12},{16,14},{18,16},{20... | collective-permute-start | bytes 393224 | tf_op jit(solution)/shard_map/while/body/eval_jaxpr/ppermute | solution.py:14
  128.7 8.7 %collective-permute-start = (f32[2,128,128]{2,1,0:T(8,128)S(1)}, f32[2,128,128]{2,1,0:T(8,128)S(1)}, u32[]{:S(2)}, u32[]{:S(2)}) collective-permute-start(f32[2,128,128]{2,1,0:T(8,128)S(1)} %convolution_add_fusion.20), channel_id=1, source_target_pairs={{2,0},{4,2},{6,4},{8,6},{10,8},{12,10},{14,12},{16,14},{18,16},{20... | collective-permute-start | bytes 393224 | tf_op jit(solution)/shard_map/while/body/eval_jaxpr/ppermute | solution.py:14
  137.6 8.7 %collective-permute-start = (f32[2,128,128]{2,1,0:T(8,128)S(1)}, f32[2,128,128]{2,1,0:T(8,128)S(1)}, u32[]{:S(2)}, u32[]{:S(2)}) collective-permute-start(f32[2,128,128]{2,1,0:T(8,128)S(1)} %convolution_add_fusion.20), channel_id=1, source_target_pairs={{2,0},{4,2},{6,4},{8,6},{10,8},{12,10},{14,12},{16,14},{18,16},{20... | collective-permute-start | bytes 393224 | tf_op jit(solution)/shard_map/while/body/eval_jaxpr/ppermute | solution.py:14
  146.5 8.7 %collective-permute-start = (f32[2,128,128]{2,1,0:T(8,128)S(1)}, f32[2,128,128]{2,1,0:T(8,128)S(1)}, u32[]{:S(2)}, u32[]{:S(2)}) collective-permute-start(f32[2,128,128]{2,1,0:T(8,128)S(1)} %convolution_add_fusion.20), channel_id=1, source_target_pairs={{2,0},{4,2},{6,4},{8,6},{10,8},{12,10},{14,12},{16,14},{18,16},{20... | collective-permute-start | bytes 393224 | tf_op jit(solution)/shard_map/while/body/eval_jaxpr/ppermute | solution.py:14
  155.5 8.8 %collective-permute-start = (f32[2,128,128]{2,1,0:T(8,128)S(1)}, f32[2,128,128]{2,1,0:T(8,128)S(1)}, u32[]{:S(2)}, u32[]{:S(2)}) collective-permute-start(f32[2,128,128]{2,1,0:T(8,128)S(1)} %convolution_add_fusion.20), channel_id=1, source_target_pairs={{2,0},{4,2},{6,4},{8,6},{10,8},{12,10},{14,12},{16,14},{18,16},{20... | collective-permute-start | bytes 393224 | tf_op jit(solution)/shard_map/while/body/eval_jaxpr/ppermute | solution.py:14
  164.3 84.2 %collective-permute-start.21 = (f32[2,2,128]{2,1,0:T(2,128)S(1)}, f32[2,2,128]{2,1,0:T(2,128)S(1)}, u32[]{:S(2)}, u32[]{:S(2)}) collective-permute-start(f32[2,2,128]{2,1,0:T(2,128)S(1)} %get-tuple-element.350), channel_id=1, source_target_pairs={{10,0},{12,2},{14,4},{16,6},{18,8},{20,10},{22,12},{24,14},{26,16}... | collective-permute-start | bytes 6152 | tf_op jit(solution)/shard_map/ppermute | solution.py:14
  249.8 9.6 %collective-permute-start.11 = (bf16[2,128,256]{1,2,0:T(8,128)(2,1)S(1)}, bf16[2,128,256]{1,2,0:T(8,128)(2,1)S(1)}, u32[]{:S(2)}, u32[]{:S(2)}) collective-permute-start(bf16[2,128,256]{1,2,0:T(8,128)(2,1)S(1)} %get-tuple-element.334), channel_id=1, source_target_pairs={{6,0},{8,2},{10,4},{12,6},{14,8},{16,10},{18,12},{20,14},{22,16},{... | collective-permute-start | bytes 393224 | tf_op jit(solution)/shard_map/ppermute | solution.py:14
  251.5 9.1 %collective-permute-start.12 = (bf16[2,128,256]{1,2,0:T(8,128)(2,1)S(1)}, bf16[2,128,256]{1,2,0:T(8,128)(2,1)S(1)}, u32[]{:S(2)}, u32[]{:S(2)}) collective-permute-start(bf16[2,128,256]{1,2,0:T(8,128)(2,1)S(1)} %get-tuple-element.334), channel_id=1, source_target_pairs={{8,0},{10,2},{12,4},{14,6},{16,8},{18,10},{20,12},{22,14},{24,16},... | collective-permute-start | bytes 393224 | tf_op jit(solution)/shard_map/ppermute | solution.py:14
  252.8 18.4 %collective-permute-start.13 = (bf16[2,128,256]{1,2,0:T(8,128)(2,1)S(1)}, bf16[2,128,256]{1,2,0:T(8,128)(2,1)S(1)}, u32[]{:S(2)}, u32[]{:S(2)}) collective-permute-start(bf16[2,128,256]{1,2,0:T(8,128)(2,1)S(1)} %get-tuple-element.334), channel_id=1, source_target_pairs={{10,0},{12,2},{14,4},{16,6},{18,8},{20,10},{22,12},{24,14},{26,16}... | collective-permute-start | bytes 393224 | tf_op jit(solution)/shard_map/ppermute | solution.py:14
  254.8 22.9 %collective-permute-start.14 = (bf16[2,128,256]{1,2,0:T(8,128)(2,1)S(1)}, bf16[2,128,256]{1,2,0:T(8,128)(2,1)S(1)}, u32[]{:S(2)}, u32[]{:S(2)}) collective-permute-start(bf16[2,128,256]{1,2,0:T(8,128)(2,1)S(1)} %get-tuple-element.334), channel_id=1, source_target_pairs={{12,0},{14,2},{16,4},{18,6},{20,8},{22,10},{24,12},{26,14},{28,16}... | collective-permute-start | bytes 393224 | tf_op jit(solution)/shard_map/ppermute | solution.py:14
  256.1 23.6 %collective-permute-start.15 = (bf16[2,128,256]{1,2,0:T(8,128)(2,1)S(1)}, bf16[2,128,256]{1,2,0:T(8,128)(2,1)S(1)}, u32[]{:S(2)}, u32[]{:S(2)}) collective-permute-start(bf16[2,128,256]{1,2,0:T(8,128)(2,1)S(1)} %get-tuple-element.334), channel_id=1, source_target_pairs={{14,0},{16,2},{18,4},{20,6},{22,8},{24,10},{26,12},{28,14},{30,16}... | collective-permute-start | bytes 393224 | tf_op jit(solution)/shard_map/ppermute | solution.py:14
  259.3 22.4 %collective-permute-start.16 = (bf16[2,128,256]{1,2,0:T(8,128)(2,1)S(1)}, bf16[2,128,256]{1,2,0:T(8,128)(2,1)S(1)}, u32[]{:S(2)}, u32[]{:S(2)}) collective-permute-start(bf16[2,128,256]{1,2,0:T(8,128)(2,1)S(1)} %get-tuple-element.334), channel_id=1, source_target_pairs={{16,0},{18,2},{20,4},{22,6},{24,8},{26,10},{28,12},{30,14},{17,1},... | collective-permute-start | bytes 393224 | tf_op jit(solution)/shard_map/ppermute | solution.py:14
  260.7 27.2 %collective-permute-start.1 = (bf16[2,128,256]{1,2,0:T(8,128)(2,1)S(1)}, bf16[2,128,256]{1,2,0:T(8,128)(2,1)}, u32[]{:S(2)}, u32[]{:S(2)}) collective-permute-start(bf16[2,128,256]{1,2,0:T(8,128)(2,1)S(1)} %pad_maximum_fusion), channel_id=1, source_target_pairs={{0,16},{2,18},{4,20},{6,22},{8,24},{10,26},{12,28},{14,30},{1,17},... | collective-permute-start | bytes 393224 | tf_op jit(solution)/shard_map/ppermute | solution.py:14
  271.3 20.5 %collective-permute-start.2 = (bf16[2,128,256]{1,2,0:T(8,128)(2,1)S(1)}, bf16[2,128,256]{1,2,0:T(8,128)(2,1)}, u32[]{:S(2)}, u32[]{:S(2)}) collective-permute-start(bf16[2,128,256]{1,2,0:T(8,128)(2,1)S(1)} %pad_maximum_fusion), channel_id=1, source_target_pairs={{0,14},{2,16},{4,18},{6,20},{8,22},{10,24},{12,26},{14,28},{16,30}... | collective-permute-start | bytes 393224 | tf_op jit(solution)/shard_map/ppermute | solution.py:14
  277.7 16.3 %collective-permute-start.3 = (bf16[2,128,256]{1,2,0:T(8,128)(2,1)S(1)}, bf16[2,128,256]{1,2,0:T(8,128)(2,1)}, u32[]{:S(2)}, u32[]{:S(2)}) collective-permute-start(bf16[2,128,256]{1,2,0:T(8,128)(2,1)S(1)} %pad_maximum_fusion), channel_id=1, source_target_pairs={{0,12},{2,14},{4,16},{6,18},{8,20},{10,22},{12,24},{14,26},{16,28}... | collective-permute-start | bytes 393224 | tf_op jit(solution)/shard_map/ppermute | solution.py:14
  279.7 18.4 %collective-permute-start.4 = (bf16[2,128,256]{1,2,0:T(8,128)(2,1)S(1)}, bf16[2,128,256]{1,2,0:T(8,128)(2,1)}, u32[]{:S(2)}, u32[]{:S(2)}) collective-permute-start(bf16[2,128,256]{1,2,0:T(8,128)(2,1)S(1)} %pad_maximum_fusion), channel_id=1, source_target_pairs={{0,10},{2,12},{4,14},{6,16},{8,18},{10,20},{12,22},{14,24},{16,26}... | collective-permute-start | bytes 393224 | tf_op jit(solution)/shard_map/ppermute | solution.py:14
  281.7 17.3 %collective-permute-start.5 = (bf16[2,128,256]{1,2,0:T(8,128)(2,1)S(1)}, bf16[2,128,256]{1,2,0:T(8,128)(2,1)}, u32[]{:S(2)}, u32[]{:S(2)}) collective-permute-start(bf16[2,128,256]{1,2,0:T(8,128)(2,1)S(1)} %pad_maximum_fusion), channel_id=1, source_target_pairs={{0,8},{2,10},{4,12},{6,14},{8,16},{10,18},{12,20},{14,22},{16,24},... | collective-permute-start | bytes 393224 | tf_op jit(solution)/shard_map/ppermute | solution.py:14
  287.8 12.1 %collective-permute-start.6 = (bf16[2,128,256]{1,2,0:T(8,128)(2,1)S(1)}, bf16[2,128,256]{1,2,0:T(8,128)(2,1)S(1)}, u32[]{:S(2)}, u32[]{:S(2)}) collective-permute-start(bf16[2,128,256]{1,2,0:T(8,128)(2,1)S(1)} %pad_maximum_fusion), channel_id=1, source_target_pairs={{0,6},{2,8},{4,10},{6,12},{8,14},{10,16},{12,18},{14,20},{16,22},{... | collective-permute-start | bytes 393224 | tf_op jit(solution)/shard_map/ppermute | solution.py:14
  291.8 8.3 %collective-permute-start.7 = (bf16[2,128,256]{1,2,0:T(8,128)(2,1)S(1)}, bf16[2,128,256]{1,2,0:T(8,128)(2,1)S(1)}, u32[]{:S(2)}, u32[]{:S(2)}) collective-permute-start(bf16[2,128,256]{1,2,0:T(8,128)(2,1)S(1)} %pad_maximum_fusion), channel_id=1, source_target_pairs={{0,4},{2,6},{4,8},{6,10},{8,12},{10,14},{12,16},{14,18},{16,20},{1... | collective-permute-start | bytes 393224 | tf_op jit(solution)/shard_map/ppermute | solution.py:14
  (41 other events, 303.9 us)
Sparse Core Ops, SparseCore 0:
  288.0 4.5 reduce-scatter.1
where the time goes:
time: 313 us; the launch traced here: 311 us
  waiting for transfers between devices  112 us (36%)
  starting transfers between devices  70.6 us (23%)
  blocking collectives  54.2 us (17%)
  matrix products  31.3 us (10%)
  local copies, waits for them, and re-layouts  19.6 us (6%)
  between operations  15.6 us (5%)
  other arithmetic  7.44 us (2%)
    ppermute x39, waiting for transfers between devices, from_behind(): return lax.ppermute(block, axis, route)  112 us
    ppermute x39, starting transfers between devices, from_behind(): return lax.ppermute(block, axis, route)  70.6 us
    all_gather x1, blocking collectives, per_device(): row_piece = lax.all_gather(w_kv, 'seq', axis=0, tiled=True)  54.2 us
    dot_general x53, matrix products, matmul(): return jnp.dot(left_side, right_side, precision=HIGH)  21.9 us
    unnamed x98, local copies, waits for them, and re-layouts  11.8 us
  transfers between devices with their start and end apart: 40, of which 17 were waited for; matrix products, arithmetic and copies ran while one was open for 16% of the time, Pallas kernels for 0%

commit v1 on v0

--- a/solution.py
+++ b/solution.py
@@ -6,6 +6,18 @@
 BLOCK = 64
 WINDOW = 1024
 HIGH = lax.Precision.HIGHEST
+
+
+def gather_by_bits(x, axis, dim):
+    ways, here = (lax.axis_size(axis), lax.axis_index(axis))
+    grown, reach = (x, 1)
+    while reach < ways:
+        theirs = lax.ppermute(grown, axis, [(d, d ^ reach) for d in range(ways)])
+        mine_first = jnp.concatenate([grown, theirs], axis=dim)
+        theirs_first = jnp.concatenate([theirs, grown], axis=dim)
+        grown = jnp.where(here & reach == 0, mine_first, theirs_first)
+        reach = 2 * reach
+    return grown
 
 
 def from_behind(block, axis, distance):
@@ -182,7 +194,7 @@
     key_grad = own_k.reshape(row_count, column_count).astype(jnp.bfloat16)
     value_grad = own_v.reshape(row_count, column_count).astype(jnp.bfloat16)
     attn_dq = grad_q.reshape(row_count, column_count).astype(jnp.bfloat16)
-    row_piece = lax.all_gather(w_kv, "seq", axis=0, tiled=True)
+    row_piece = gather_by_bits(w_kv, "seq", 0)
     from_keys = lax.dot_general(
         row_piece[:, 0, :], key_grad, (((1,), (1,)), ((), ())), preferred_element_type=jnp.float32
     )

time: 313 us -> 302 us (0.965)
  blocking collectives: 54.2 us -> 0 us
  waiting for transfers between devices: 112 us -> 141 us
  starting transfers between devices: 70.6 us -> 82.4 us
  local copies, waits for them, and re-layouts: 19.6 us -> 16.3 us
  other arithmetic: 7.44 us -> 10.7 us
    all_gather x1 -> x0, blocking collectives: 54.2 us -> none  [per_device(): row_piece = lax.all_gather(w_kv, 'seq', axis=0, tiled=True)]
    ppermute x0 -> x4, waiting for transfers between devices: none -> 15.5 us  [gather_by_bits(): theirs = lax.ppermute(grown, axis, [(d, d ^ reach) for d in range(ways)])]
    ppermute x39, waiting for transfers between devices: 112 us -> 121 us  [from_behind(): return lax.ppermute(block, axis, route)]
    ppermute x0 -> x4, starting transfers between devices: none -> 8.16 us  [gather_by_bits(): theirs = lax.ppermute(grown, axis, [(d, d ^ reach) for d in range(ways)])]
    reduce_scatter x1, waiting for transfers between devices: 0.01 us -> 5.27 us  [per_device(): lax.psum_scatter(partial_value, 'head', scatter_dimension=0, tiled=True)]
    ppermute x39, starting transfers between devices: 70.6 us -> 74.2 us  [from_behind(): return lax.ppermute(block, axis, route)]
    unnamed x98 -> x113, local copies, waits for them, and re-layouts: 11.8 us -> 9.1 us
  transfers between devices with their start and end apart: 40 -> 44, of which waited for: 17 -> 22; matrix products, arithmetic and copies ran while one was open for 16% -> 17% of each run, Pallas kernels for 0% -> 0%
where the time goes in v1:
time: 302 us; the launch traced here: 300 us
  waiting for transfers between devices  141 us (47%)
  starting transfers between devices  82.4 us (27%)
  matrix products  33.3 us (11%)
  local copies, waits for them, and re-layouts  16.3 us (5%)
  between operations  15.7 us (5%)
  other arithmetic  10.7 us (4%)
    ppermute x39, waiting for transfers between devices, from_behind(): return lax.ppermute(block, axis, route)  121 us
    ppermute x39, starting transfers between devices, from_behind(): return lax.ppermute(block, axis, route)  74.2 us
    dot_general x53, matrix products, matmul(): return jnp.dot(left_side, right_side, precision=HIGH)  22.4 us
    ppermute x4, waiting for transfers between devices, gather_by_bits(): theirs = lax.ppermute(grown, axis, [(d, d ^ reach) for d in range(ways)])  15.5 us
    unnamed x113, local copies, waits for them, and re-layouts  9.1 us
    ppermute x4, starting transfers between devices, gather_by_bits(): theirs = lax.ppermute(grown, axis, [(d, d ^ reach) for d in range(ways)])  8.16 us
  transfers between devices with their start and end apart: 44, of which 22 were waited for; matrix products, arithmetic and copies ran while one was open for 17% of the time, Pallas kernels for 0%

profile of v1, /device:TPU:0, one launch (start us, length us, event | category | flops | bytes accessed | tf_op | source)
XLA Modules:
  0.0 300.3 jit_solution(8211843702752108470)
XLA Ops:
  26.0 1.9 fusion.49
  32.0 133.4 %while.43 = (s32[]{:T(128)}, f32[2,128,128]{2,1,0:T(8,128)S(1)}, f32[2,128,128]{2,1,0:T(8,128)S(1)}, f32[2,128,128]{2,1,0:T(8,128)S(1)}, s32[]{:T(128)}) while((s32[]{:T(128)}, f32[2,128,128]{2,1,0:T(8,128)S(1)}, f32[2,128,128]{2,1,0:T(8,128)S(1)}, f32[2,128,128]{2,1,0:T(8,128)S(1)}, s32[]{:T(128)}) %tuple.116), condition=%wide.region_9.10_spmd, body=%wide.region_8.9_spmd.sunk | while | flops 50364416 | bytes 1048677 | solution.py:245
  33.6 7.7 %collective-permute-done = f32[2,128,128]{2,1,0:T(8,128)S(1)} collective-permute-done((f32[2,128,128]{2,1,0:T(8,128)S(1)}, f32[2,128,128]{2,1,0:T(8,128)S(1)}, u32[]{:S(2)}, u32[]{:S(2)}) %collective-permute-start) | collective-permute-done | bytes 131104 | tf_op jit(solution)/shard_map/while/body/eval_jaxpr/ppermute | solution.py:26
  42.9 6.8 %collective-permute-done = f32[2,128,128]{2,1,0:T(8,128)S(1)} collective-permute-done((f32[2,128,128]{2,1,0:T(8,128)S(1)}, f32[2,128,128]{2,1,0:T(8,128)S(1)}, u32[]{:S(2)}, u32[]{:S(2)}) %collective-permute-start) | collective-permute-done | bytes 131104 | tf_op jit(solution)/shard_map/while/body/eval_jaxpr/ppermute | solution.py:26
  51.3 6.5 %collective-permute-done = f32[2,128,128]{2,1,0:T(8,128)S(1)} collective-permute-done((f32[2,128,128]{2,1,0:T(8,128)S(1)}, f32[2,128,128]{2,1,0:T(8,128)S(1)}, u32[]{:S(2)}, u32[]{:S(2)}) %collective-permute-start) | collective-permute-done | bytes 131104 | tf_op jit(solution)/shard_map/while/body/eval_jaxpr/ppermute | solution.py:26
  59.3 6.5 %collective-permute-done = f32[2,128,128]{2,1,0:T(8,128)S(1)} collective-permute-done((f32[2,128,128]{2,1,0:T(8,128)S(1)}, f32[2,128,128]{2,1,0:T(8,128)S(1)}, u32[]{:S(2)}, u32[]{:S(2)}) %collective-permute-start) | collective-permute-done | bytes 131104 | tf_op jit(solution)/shard_map/while/body/eval_jaxpr/ppermute | solution.py:26
  67.4 6.9 %collective-permute-done = f32[2,128,128]{2,1,0:T(8,128)S(1)} collective-permute-done((f32[2,128,128]{2,1,0:T(8,128)S(1)}, f32[2,128,128]{2,1,0:T(8,128)S(1)}, u32[]{:S(2)}, u32[]{:S(2)}) %collective-permute-start) | collective-permute-done | bytes 131104 | tf_op jit(solution)/shard_map/while/body/eval_jaxpr/ppermute | solution.py:26
  75.8 7.4 %collective-permute-done = f32[2,128,128]{2,1,0:T(8,128)S(1)} collective-permute-done((f32[2,128,128]{2,1,0:T(8,128)S(1)}, f32[2,128,128]{2,1,0:T(8,128)S(1)}, u32[]{:S(2)}, u32[]{:S(2)}) %collective-permute-start) | collective-permute-done | bytes 131104 | tf_op jit(solution)/shard_map/while/body/eval_jaxpr/ppermute | solution.py:26
  84.8 8.7 %collective-permute-done = f32[2,128,128]{2,1,0:T(8,128)S(1)} collective-permute-done((f32[2,128,128]{2,1,0:T(8,128)S(1)}, f32[2,128,128]{2,1,0:T(8,128)S(1)}, u32[]{:S(2)}, u32[]{:S(2)}) %collective-permute-start) | collective-permute-done | bytes 131104 | tf_op jit(solution)/shard_map/while/body/eval_jaxpr/ppermute | solution.py:26
  95.0 8.8 %collective-permute-done = f32[2,128,128]{2,1,0:T(8,128)S(1)} collective-permute-done((f32[2,128,128]{2,1,0:T(8,128)S(1)}, f32[2,128,128]{2,1,0:T(8,128)S(1)}, u32[]{:S(2)}, u32[]{:S(2)}) %collective-permute-start) | collective-permute-done | bytes 131104 | tf_op jit(solution)/shard_map/while/body/eval_jaxpr/ppermute | solution.py:26
  105.3 7.2 %collective-permute-done = f32[2,128,128]{2,1,0:T(8,128)S(1)} collective-permute-done((f32[2,128,128]{2,1,0:T(8,128)S(1)}, f32[2,128,128]{2,1,0:T(8,128)S(1)}, u32[]{:S(2)}, u32[]{:S(2)}) %collective-permute-start) | collective-permute-done | bytes 131104 | tf_op jit(solution)/shard_map/while/body/eval_jaxpr/ppermute | solution.py:26
  114.1 6.8 %collective-permute-done = f32[2,128,128]{2,1,0:T(8,128)S(1)} collective-permute-done((f32[2,128,128]{2,1,0:T(8,128)S(1)}, f32[2,128,128]{2,1,0:T(8,128)S(1)}, u32[]{:S(2)}, u32[]{:S(2)}) %collective-permute-start) | collective-permute-done | bytes 131104 | tf_op jit(solution)/shard_map/while/body/eval_jaxpr/ppermute | solution.py:26
  122.5 7.1 %collective-permute-done = f32[2,128,128]{2,1,0:T(8,128)S(1)} collective-permute-done((f32[2,128,128]{2,1,0:T(8,128)S(1)}, f32[2,128,128]{2,1,0:T(8,128)S(1)}, u32[]{:S(2)}, u32[]{:S(2)}) %collective-permute-start) | collective-permute-done | bytes 131104 | tf_op jit(solution)/shard_map/while/body/eval_jaxpr/ppermute | solution.py:26
  131.1 7.4 %collective-permute-done = f32[2,128,128]{2,1,0:T(8,128)S(1)} collective-permute-done((f32[2,128,128]{2,1,0:T(8,128)S(1)}, f32[2,128,128]{2,1,0:T(8,128)S(1)}, u32[]{:S(2)}, u32[]{:S(2)}) %collective-permute-start) | collective-permute-done | bytes 131104 | tf_op jit(solution)/shard_map/while/body/eval_jaxpr/ppermute | solution.py:26
  140.0 7.4 %collective-permute-done = f32[2,128,128]{2,1,0:T(8,128)S(1)} collective-permute-done((f32[2,128,128]{2,1,0:T(8,128)S(1)}, f32[2,128,128]{2,1,0:T(8,128)S(1)}, u32[]{:S(2)}, u32[]{:S(2)}) %collective-permute-start) | collective-permute-done | bytes 131104 | tf_op jit(solution)/shard_map/while/body/eval_jaxpr/ppermute | solution.py:26
  149.0 7.4 %collective-permute-done = f32[2,128,128]{2,1,0:T(8,128)S(1)} collective-permute-done((f32[2,128,128]{2,1,0:T(8,128)S(1)}, f32[2,128,128]{2,1,0:T(8,128)S(1)}, u32[]{:S(2)}, u32[]{:S(2)}) %collective-permute-start) | collective-permute-done | bytes 131104 | tf_op jit(solution)/shard_map/while/body/eval_jaxpr/ppermute | solution.py:26
  157.9 7.5 %collective-permute-done = f32[2,128,128]{2,1,0:T(8,128)S(1)} collective-permute-done((f32[2,128,128]{2,1,0:T(8,128)S(1)}, f32[2,128,128]{2,1,0:T(8,128)S(1)}, u32[]{:S(2)}, u32[]{:S(2)}) %collective-permute-start) | collective-permute-done | bytes 131104 | tf_op jit(solution)/shard_map/while/body/eval_jaxpr/ppermute | solution.py:26
  199.9 5.5 %collective-permute-done.26 = f32[2,2,128]{2,1,0:T(2,128)S(1)} collective-permute-done((f32[2,2,128]{2,1,0:T(2,128)}, f32[2,2,128]{2,1,0:T(2,128)S(1)}, u32[]{:S(2)}, u32[]{:S(2)}) %collective-permute-start.26) | collective-permute-done | bytes 2080 | tf_op jit(solution)/shard_map/ppermute | solution.py:26
  206.7 4.5 %collective-permute-done.27 = f32[2,2,128]{2,1,0:T(2,128)S(1)} collective-permute-done((f32[2,2,128]{2,1,0:T(2,128)}, f32[2,2,128]{2,1,0:T(2,128)S(1)}, u32[]{:S(2)}, u32[]{:S(2)}) %collective-permute-start.27) | collective-permute-done | bytes 2080 | tf_op jit(solution)/shard_map/ppermute | solution.py:26
  212.7 4.9 %collective-permute-done.9 = bf16[32,2,256]{2,0,1:T(8,128)(2,1)S(1)} collective-permute-done((bf16[32,2,256]{2,0,1:T(8,128)(2,1)S(1)}, bf16[32,2,256]{2,0,1:T(8,128)(2,1)S(1)}, u32[]{:S(2)}, u32[]{:S(2)}) %collective-permute-start.9) | collective-permute-done | bytes 32800 | tf_op jit(solution)/shard_map/ppermute | solution.py:15
  218.1 3.8 %collective-permute-done.10 = bf16[64,2,256]{2,0,1:T(8,128)(2,1)S(1)} collective-permute-done((bf16[64,2,256]{2,0,1:T(8,128)(2,1)S(1)}, bf16[64,2,256]{2,0,1:T(8,128)(2,1)S(1)}, u32[]{:S(2)}, u32[]{:S(2)}) %collective-permute-start.10) | collective-permute-done | bytes 65568 | tf_op jit(solution)/shard_map/ppermute | solution.py:15
  227.9 14.8 %collective-permute-start.1 = (bf16[2,128,256]{1,2,0:T(8,128)(2,1)}, bf16[2,128,256]{1,2,0:T(8,128)(2,1)S(1)}, u32[]{:S(2)}, u32[]{:S(2)}) collective-permute-start(bf16[2,128,256]{1,2,0:T(8,128)(2,1)} %pad_maximum_fusion), channel_id=1, source_target_pairs={{0,16},{2,18},{4,20},{6,22},{8,24},{10,26},{12,28},{14,30},{1,17},... | collective-permute-start | bytes 393224 | tf_op jit(solution)/shard_map/ppermute | solution.py:26
  242.8 5.7 %collective-permute-start.2 = (bf16[2,128,256]{1,2,0:T(8,128)(2,1)}, bf16[2,128,256]{1,2,0:T(8,128)(2,1)S(1)}, u32[]{:S(2)}, u32[]{:S(2)}) collective-permute-start(bf16[2,128,256]{1,2,0:T(8,128)(2,1)} %pad_maximum_fusion), channel_id=1, source_target_pairs={{0,14},{2,16},{4,18},{6,20},{8,22},{10,24},{12,26},{14,28},{16,30}... | collective-permute-start | bytes 393224 | tf_op jit(solution)/shard_map/ppermute | solution.py:26
  251.3 2.5 collective-permute-start.5
  254.0 3.9 %collective-permute-start.6 = (bf16[2,128,256]{1,2,0:T(8,128)(2,1)}, bf16[2,128,256]{1,2,0:T(8,128)(2,1)S(1)}, u32[]{:S(2)}, u32[]{:S(2)}) collective-permute-start(bf16[2,128,256]{1,2,0:T(8,128)(2,1)} %pad_maximum_fusion), channel_id=1, source_target_pairs={{0,6},{2,8},{4,10},{6,12},{8,14},{10,16},{12,18},{14,20},{16,22},{... | collective-permute-start | bytes 393224 | tf_op jit(solution)/shard_map/ppermute | solution.py:26
  257.9 1.6 collective-permute-start.7
  259.5 2.8 collective-permute-start.8
  262.4 1.8 collective-permute-start.11
  266.7 2.2 fusion.33
  270.1 5.8 %collective-permute-start.12 = (bf16[256,2,256]{2,0,1:T(8,128)(2,1)S(1)}, bf16[256,2,256]{2,0,1:T(8,128)(2,1)S(1)}, u32[]{:S(2)}, u32[]{:S(2)}) collective-permute-start(bf16[256,2,256]{2,0,1:T(8,128)(2,1)S(1)} %maximum_select_fusion.1), channel_id=1, source_target_pairs={{0,16},{2,18},{4,20},{6,22},{8,24},{10,26},{12,28},{14,30},{16,0},... | collective-permute-start | bytes 786440 | tf_op jit(solution)/shard_map/ppermute | solution.py:15
  276.3 6.8 %collective-permute-done.12 = bf16[256,2,256]{2,0,1:T(8,128)(2,1)S(1)} collective-permute-done((bf16[256,2,256]{2,0,1:T(8,128)(2,1)S(1)}, bf16[256,2,256]{2,0,1:T(8,128)(2,1)S(1)}, u32[]{:S(2)}, u32[]{:S(2)}) %collective-permute-start.12) | collective-permute-done | bytes 262176 | tf_op jit(solution)/shard_map/ppermute | solution.py:15
  286.7 5.3 %reduce-scatter.2.cloned.1.call-done = f32[256,128]{1,0:T(8,128)} async-done(((f32[512,128]{1,0:T(8,128)}), f32[256,128]{1,0:T(8,128)}) %reduce-scatter.2.cloned.1.call-update) | async-done | bytes 131088 | tf_op jit(solution)/shard_map/reduce_scatter | solution.py:204
  (333 shorter events, 102.6 us)
Async XLA Ops:
  7.2 284.8 %reduce-scatter.2.cloned.1.call-start = ((), (), s32[]{:S(2)}) async-start(), calls=%async_computation.1 | async-start | bytes 393216 | tf_op jit(solution)/shard_map/reduce_scatter | solution.py:204
  10.6 179.3 %collective-permute-start.21 = (f32[2,2,128]{2,1,0:T(2,128)}, f32[2,2,128]{2,1,0:T(2,128)}, u32[]{:S(2)}, u32[]{:S(2)}) collective-permute-start(f32[2,2,128]{2,1,0:T(2,128)} %get-tuple-element.350), channel_id=1, source_target_pairs={{2,0},{4,2},{6,4},{8,6},{10,8},{12,10},{14,12},{16,14},{18,16},{20... | collective-permute-start | bytes 6152 | tf_op jit(solution)/shard_map/ppermute | solution.py:26
  11.9 180.0 %collective-permute-start.22 = (f32[2,2,128]{2,1,0:T(2,128)}, f32[2,2,128]{2,1,0:T(2,128)}, u32[]{:S(2)}, u32[]{:S(2)}) collective-permute-start(f32[2,2,128]{2,1,0:T(2,128)} %get-tuple-element.350), channel_id=1, source_target_pairs={{4,0},{6,2},{8,4},{10,6},{12,8},{14,10},{16,12},{18,14},{20,16},{2... | collective-permute-start | bytes 6152 | tf_op jit(solution)/shard_map/ppermute | solution.py:26
  13.2 180.7 %collective-permute-start.23 = (f32[2,2,128]{2,1,0:T(2,128)}, f32[2,2,128]{2,1,0:T(2,128)}, u32[]{:S(2)}, u32[]{:S(2)}) collective-permute-start(f32[2,2,128]{2,1,0:T(2,128)} %get-tuple-element.350), channel_id=1, source_target_pairs={{6,0},{8,2},{10,4},{12,6},{14,8},{16,10},{18,12},{20,14},{22,16},{... | collective-permute-start | bytes 6152 | tf_op jit(solution)/shard_map/ppermute | solution.py:26
  14.5 181.5 %collective-permute-start.24 = (f32[2,2,128]{2,1,0:T(2,128)}, f32[2,2,128]{2,1,0:T(2,128)}, u32[]{:S(2)}, u32[]{:S(2)}) collective-permute-start(f32[2,2,128]{2,1,0:T(2,128)} %get-tuple-element.350), channel_id=1, source_target_pairs={{8,0},{10,2},{12,4},{14,6},{16,8},{18,10},{20,12},{22,14},{24,16},... | collective-permute-start | bytes 6152 | tf_op jit(solution)/shard_map/ppermute | solution.py:26
  32.3 9.0 %collective-permute-start = (f32[2,128,128]{2,1,0:T(8,128)S(1)}, f32[2,128,128]{2,1,0:T(8,128)S(1)}, u32[]{:S(2)}, u32[]{:S(2)}) collective-permute-start(f32[2,128,128]{2,1,0:T(8,128)S(1)} %convolution_add_fusion.20), channel_id=1, source_target_pairs={{2,0},{4,2},{6,4},{8,6},{10,8},{12,10},{14,12},{16,14},{18,16},{20... | collective-permute-start | bytes 393224 | tf_op jit(solution)/shard_map/while/body/eval_jaxpr/ppermute | solution.py:26
  74.5 8.7 %collective-permute-start = (f32[2,128,128]{2,1,0:T(8,128)S(1)}, f32[2,128,128]{2,1,0:T(8,128)S(1)}, u32[]{:S(2)}, u32[]{:S(2)}) collective-permute-start(f32[2,128,128]{2,1,0:T(8,128)S(1)} %convolution_add_fusion.20), channel_id=1, source_target_pairs={{2,0},{4,2},{6,4},{8,6},{10,8},{12,10},{14,12},{16,14},{18,16},{20... | collective-permute-start | bytes 393224 | tf_op jit(solution)/shard_map/while/body/eval_jaxpr/ppermute | solution.py:26
  83.5 10.0 %collective-permute-start = (f32[2,128,128]{2,1,0:T(8,128)S(1)}, f32[2,128,128]{2,1,0:T(8,128)S(1)}, u32[]{:S(2)}, u32[]{:S(2)}) collective-permute-start(f32[2,128,128]{2,1,0:T(8,128)S(1)} %convolution_add_fusion.20), channel_id=1, source_target_pairs={{2,0},{4,2},{6,4},{8,6},{10,8},{12,10},{14,12},{16,14},{18,16},{20... | collective-permute-start | bytes 393224 | tf_op jit(solution)/shard_map/while/body/eval_jaxpr/ppermute | solution.py:26
  93.7 10.1 %collective-permute-start = (f32[2,128,128]{2,1,0:T(8,128)S(1)}, f32[2,128,128]{2,1,0:T(8,128)S(1)}, u32[]{:S(2)}, u32[]{:S(2)}) collective-permute-start(f32[2,128,128]{2,1,0:T(8,128)S(1)} %convolution_add_fusion.20), channel_id=1, source_target_pairs={{2,0},{4,2},{6,4},{8,6},{10,8},{12,10},{14,12},{16,14},{18,16},{20... | collective-permute-start | bytes 393224 | tf_op jit(solution)/shard_map/while/body/eval_jaxpr/ppermute | solution.py:26
  129.8 8.7 %collective-permute-start = (f32[2,128,128]{2,1,0:T(8,128)S(1)}, f32[2,128,128]{2,1,0:T(8,128)S(1)}, u32[]{:S(2)}, u32[]{:S(2)}) collective-permute-start(f32[2,128,128]{2,1,0:T(8,128)S(1)} %convolution_add_fusion.20), channel_id=1, source_target_pairs={{2,0},{4,2},{6,4},{8,6},{10,8},{12,10},{14,12},{16,14},{18,16},{20... | collective-permute-start | bytes 393224 | tf_op jit(solution)/shard_map/while/body/eval_jaxpr/ppermute | solution.py:26
  138.7 8.7 %collective-permute-start = (f32[2,128,128]{2,1,0:T(8,128)S(1)}, f32[2,128,128]{2,1,0:T(8,128)S(1)}, u32[]{:S(2)}, u32[]{:S(2)}) collective-permute-start(f32[2,128,128]{2,1,0:T(8,128)S(1)} %convolution_add_fusion.20), channel_id=1, source_target_pairs={{2,0},{4,2},{6,4},{8,6},{10,8},{12,10},{14,12},{16,14},{18,16},{20... | collective-permute-start | bytes 393224 | tf_op jit(solution)/shard_map/while/body/eval_jaxpr/ppermute | solution.py:26
  147.7 8.7 %collective-permute-start = (f32[2,128,128]{2,1,0:T(8,128)S(1)}, f32[2,128,128]{2,1,0:T(8,128)S(1)}, u32[]{:S(2)}, u32[]{:S(2)}) collective-permute-start(f32[2,128,128]{2,1,0:T(8,128)S(1)} %convolution_add_fusion.20), channel_id=1, source_target_pairs={{2,0},{4,2},{6,4},{8,6},{10,8},{12,10},{14,12},{16,14},{18,16},{20... | collective-permute-start | bytes 393224 | tf_op jit(solution)/shard_map/while/body/eval_jaxpr/ppermute | solution.py:26
  156.6 8.8 %collective-permute-start = (f32[2,128,128]{2,1,0:T(8,128)S(1)}, f32[2,128,128]{2,1,0:T(8,128)S(1)}, u32[]{:S(2)}, u32[]{:S(2)}) collective-permute-start(f32[2,128,128]{2,1,0:T(8,128)S(1)} %convolution_add_fusion.20), channel_id=1, source_target_pairs={{2,0},{4,2},{6,4},{8,6},{10,8},{12,10},{14,12},{16,14},{18,16},{20... | collective-permute-start | bytes 393224 | tf_op jit(solution)/shard_map/while/body/eval_jaxpr/ppermute | solution.py:26
  165.4 32.5 %collective-permute-start.25 = (f32[2,2,128]{2,1,0:T(2,128)}, f32[2,2,128]{2,1,0:T(2,128)}, u32[]{:S(2)}, u32[]{:S(2)}) collective-permute-start(f32[2,2,128]{2,1,0:T(2,128)} %get-tuple-element.350), channel_id=1, source_target_pairs={{10,0},{12,2},{14,4},{16,6},{18,8},{20,10},{22,12},{24,14},{26,16}... | collective-permute-start | bytes 6152 | tf_op jit(solution)/shard_map/ppermute | solution.py:26
  189.8 15.6 %collective-permute-start.26 = (f32[2,2,128]{2,1,0:T(2,128)}, f32[2,2,128]{2,1,0:T(2,128)S(1)}, u32[]{:S(2)}, u32[]{:S(2)}) collective-permute-start(f32[2,2,128]{2,1,0:T(2,128)} %get-tuple-element.350), channel_id=1, source_target_pairs={{12,0},{14,2},{16,4},{18,6},{20,8},{22,10},{24,12},{26,14},{28,16}... | collective-permute-start | bytes 6152 | tf_op jit(solution)/shard_map/ppermute | solution.py:26
  191.8 19.4 %collective-permute-start.27 = (f32[2,2,128]{2,1,0:T(2,128)}, f32[2,2,128]{2,1,0:T(2,128)S(1)}, u32[]{:S(2)}, u32[]{:S(2)}) collective-permute-start(f32[2,2,128]{2,1,0:T(2,128)} %get-tuple-element.350), channel_id=1, source_target_pairs={{14,0},{16,2},{18,4},{20,6},{22,8},{24,10},{26,12},{28,14},{30,16}... | collective-permute-start | bytes 6152 | tf_op jit(solution)/shard_map/ppermute | solution.py:26
  193.8 18.8 %collective-permute-start.28 = (f32[2,2,128]{2,1,0:T(2,128)}, f32[2,2,128]{2,1,0:T(2,128)S(1)}, u32[]{:S(2)}, u32[]{:S(2)}) collective-permute-start(f32[2,2,128]{2,1,0:T(2,128)} %get-tuple-element.350), channel_id=1, source_target_pairs={{16,0},{18,2},{20,4},{22,6},{24,8},{26,10},{28,12},{30,14},{17,1},... | collective-permute-start | bytes 6152 | tf_op jit(solution)/shard_map/ppermute | solution.py:26
  196.0 27.9 %collective-permute-start.13 = (bf16[2,128,256]{1,2,0:T(8,128)(2,1)S(1)}, bf16[2,128,256]{1,2,0:T(8,128)(2,1)S(1)}, u32[]{:S(2)}, u32[]{:S(2)}) collective-permute-start(bf16[2,128,256]{1,2,0:T(8,128)(2,1)S(1)} %get-tuple-element.334), channel_id=1, source_target_pairs={{2,0},{4,2},{6,4},{8,6},{10,8},{12,10},{14,12},{16,14},{18,16},{20... | collective-permute-start | bytes 393224 | tf_op jit(solution)/shard_map/ppermute | solution.py:26
  198.0 27.2 %collective-permute-start.14 = (bf16[2,128,256]{1,2,0:T(8,128)(2,1)S(1)}, bf16[2,128,256]{1,2,0:T(8,128)(2,1)S(1)}, u32[]{:S(2)}, u32[]{:S(2)}) collective-permute-start(bf16[2,128,256]{1,2,0:T(8,128)(2,1)S(1)} %get-tuple-element.334), channel_id=1, source_target_pairs={{4,0},{6,2},{8,4},{10,6},{12,8},{14,10},{16,12},{18,14},{20,16},{2... | collective-permute-start | bytes 393224 | tf_op jit(solution)/shard_map/ppermute | solution.py:26
  205.4 21.1 %collective-permute-start.15 = (bf16[2,128,256]{1,2,0:T(8,128)(2,1)S(1)}, bf16[2,128,256]{1,2,0:T(8,128)(2,1)S(1)}, u32[]{:S(2)}, u32[]{:S(2)}) collective-permute-start(bf16[2,128,256]{1,2,0:T(8,128)(2,1)S(1)} %get-tuple-element.334), channel_id=1, source_target_pairs={{6,0},{8,2},{10,4},{12,6},{14,8},{16,10},{18,12},{20,14},{22,16},{... | collective-permute-start | bytes 393224 | tf_op jit(solution)/shard_map/ppermute | solution.py:26
  211.3 16.6 %collective-permute-start.16 = (bf16[2,128,256]{1,2,0:T(8,128)(2,1)S(1)}, bf16[2,128,256]{1,2,0:T(8,128)(2,1)S(1)}, u32[]{:S(2)}, u32[]{:S(2)}) collective-permute-start(bf16[2,128,256]{1,2,0:T(8,128)(2,1)S(1)} %get-tuple-element.334), channel_id=1, source_target_pairs={{8,0},{10,2},{12,4},{14,6},{16,8},{18,10},{20,12},{22,14},{24,16},... | collective-permute-start | bytes 393224 | tf_op jit(solution)/shard_map/ppermute | solution.py:26
  221.9 20.9 %collective-permute-start.17 = (bf16[2,128,256]{1,2,0:T(8,128)(2,1)S(1)}, bf16[2,128,256]{1,2,0:T(8,128)(2,1)S(1)}, u32[]{:S(2)}, u32[]{:S(2)}) collective-permute-start(bf16[2,128,256]{1,2,0:T(8,128)(2,1)S(1)} %get-tuple-element.334), channel_id=1, source_target_pairs={{10,0},{12,2},{14,4},{16,6},{18,8},{20,10},{22,12},{24,14},{26,16}... | collective-permute-start | bytes 393224 | tf_op jit(solution)/shard_map/ppermute | solution.py:26
  223.9 24.7 %collective-permute-start.18 = (bf16[2,128,256]{1,2,0:T(8,128)(2,1)S(1)}, bf16[2,128,256]{1,2,0:T(8,128)(2,1)S(1)}, u32[]{:S(2)}, u32[]{:S(2)}) collective-permute-start(bf16[2,128,256]{1,2,0:T(8,128)(2,1)S(1)} %get-tuple-element.334), channel_id=1, source_target_pairs={{12,0},{14,2},{16,4},{18,6},{20,8},{22,10},{24,12},{26,14},{28,16}... | collective-permute-start | bytes 393224 | tf_op jit(solution)/shard_map/ppermute | solution.py:26
  225.2 24.7 %collective-permute-start.19 = (bf16[2,128,256]{1,2,0:T(8,128)(2,1)S(1)}, bf16[2,128,256]{1,2,0:T(8,128)(2,1)S(1)}, u32[]{:S(2)}, u32[]{:S(2)}) collective-permute-start(bf16[2,128,256]{1,2,0:T(8,128)(2,1)S(1)} %get-tuple-element.334), channel_id=1, source_target_pairs={{14,0},{16,2},{18,4},{20,6},{22,8},{24,10},{26,12},{28,14},{30,16}... | collective-permute-start | bytes 393224 | tf_op jit(solution)/shard_map/ppermute | solution.py:26
  226.6 24.7 %collective-permute-start.20 = (bf16[2,128,256]{1,2,0:T(8,128)(2,1)S(1)}, bf16[2,128,256]{1,2,0:T(8,128)(2,1)S(1)}, u32[]{:S(2)}, u32[]{:S(2)}) collective-permute-start(bf16[2,128,256]{1,2,0:T(8,128)(2,1)S(1)} %get-tuple-element.334), channel_id=1, source_target_pairs={{16,0},{18,2},{20,4},{22,6},{24,8},{26,10},{28,12},{30,14},{17,1},... | collective-permute-start | bytes 393224 | tf_op jit(solution)/shard_map/ppermute | solution.py:26
  227.9 26.0 %collective-permute-start.1 = (bf16[2,128,256]{1,2,0:T(8,128)(2,1)}, bf16[2,128,256]{1,2,0:T(8,128)(2,1)S(1)}, u32[]{:S(2)}, u32[]{:S(2)}) collective-permute-start(bf16[2,128,256]{1,2,0:T(8,128)(2,1)} %pad_maximum_fusion), channel_id=1, source_target_pairs={{0,16},{2,18},{4,20},{6,22},{8,24},{10,26},{12,28},{14,30},{1,17},... | collective-permute-start | bytes 393224 | tf_op jit(solution)/shard_map/ppermute | solution.py:26
  242.8 15.0 %collective-permute-start.2 = (bf16[2,128,256]{1,2,0:T(8,128)(2,1)}, bf16[2,128,256]{1,2,0:T(8,128)(2,1)S(1)}, u32[]{:S(2)}, u32[]{:S(2)}) collective-permute-start(bf16[2,128,256]{1,2,0:T(8,128)(2,1)} %pad_maximum_fusion), channel_id=1, source_target_pairs={{0,14},{2,16},{4,18},{6,20},{8,22},{10,24},{12,26},{14,28},{16,30}... | collective-permute-start | bytes 393224 | tf_op jit(solution)/shard_map/ppermute | solution.py:26
  248.6 10.9 %collective-permute-start.3 = (bf16[2,128,256]{1,2,0:T(8,128)(2,1)}, bf16[2,128,256]{1,2,0:T(8,128)(2,1)S(1)}, u32[]{:S(2)}, u32[]{:S(2)}) collective-permute-start(bf16[2,128,256]{1,2,0:T(8,128)(2,1)} %pad_maximum_fusion), channel_id=1, source_target_pairs={{0,12},{2,14},{4,16},{6,18},{8,20},{10,22},{12,24},{14,26},{16,28}... | collective-permute-start | bytes 393224 | tf_op jit(solution)/shard_map/ppermute | solution.py:26
  250.0 12.4 %collective-permute-start.4 = (bf16[2,128,256]{1,2,0:T(8,128)(2,1)}, bf16[2,128,256]{1,2,0:T(8,128)(2,1)S(1)}, u32[]{:S(2)}, u32[]{:S(2)}) collective-permute-start(bf16[2,128,256]{1,2,0:T(8,128)(2,1)} %pad_maximum_fusion), channel_id=1, source_target_pairs={{0,10},{2,12},{4,14},{6,16},{8,18},{10,20},{12,22},{14,24},{16,26}... | collective-permute-start | bytes 393224 | tf_op jit(solution)/shard_map/ppermute | solution.py:26
  251.3 12.9 %collective-permute-start.5 = (bf16[2,128,256]{1,2,0:T(8,128)(2,1)}, bf16[2,128,256]{1,2,0:T(8,128)(2,1)S(1)}, u32[]{:S(2)}, u32[]{:S(2)}) collective-permute-start(bf16[2,128,256]{1,2,0:T(8,128)(2,1)} %pad_maximum_fusion), channel_id=1, source_target_pairs={{0,8},{2,10},{4,12},{6,14},{8,16},{10,18},{12,20},{14,22},{16,24},... | collective-permute-start | bytes 393224 | tf_op jit(solution)/shard_map/ppermute | solution.py:26
  254.0 10.3 %collective-permute-start.6 = (bf16[2,128,256]{1,2,0:T(8,128)(2,1)}, bf16[2,128,256]{1,2,0:T(8,128)(2,1)S(1)}, u32[]{:S(2)}, u32[]{:S(2)}) collective-permute-start(bf16[2,128,256]{1,2,0:T(8,128)(2,1)} %pad_maximum_fusion), channel_id=1, source_target_pairs={{0,6},{2,8},{4,10},{6,12},{8,14},{10,16},{12,18},{14,20},{16,22},{... | collective-permute-start | bytes 393224 | tf_op jit(solution)/shard_map/ppermute | solution.py:26
  270.1 13.0 %collective-permute-start.12 = (bf16[256,2,256]{2,0,1:T(8,128)(2,1)S(1)}, bf16[256,2,256]{2,0,1:T(8,128)(2,1)S(1)}, u32[]{:S(2)}, u32[]{:S(2)}) collective-permute-start(bf16[256,2,256]{2,0,1:T(8,128)(2,1)S(1)} %maximum_select_fusion.1), channel_id=1, source_target_pairs={{0,16},{2,18},{4,20},{6,22},{8,24},{10,26},{12,28},{14,30},{16,0},... | collective-permute-start | bytes 786440 | tf_op jit(solution)/shard_map/ppermute | solution.py:15
  (53 other events, 237.7 us)
Sparse Core Ops, SparseCore 0:
  284.6 7.3 reduce-scatter.1
